TPU v7x, 32 devices: a whole 2x2x4 slice. The times are simulated.
32 devices in a mesh: groups: 2 (over y), tm: 4 (over z), head: 4 (over x, core).
Axes of the slice: x: 2, y: 2, z: 4, core: 2. Of those that a mesh axis runs over, the one named last changes fastest.
Arguments:
- queries: bfloat16 [8, 256, 3072], P(('groups', 'tm'), 'head'), parts along dimension 0, may hold values from -128 to 128
- keys: bfloat16 [8, 256, 3072], P(('groups', 'tm'), 'head'), parts along dimension 0, may hold values from -6 to 6
- values: bfloat16 [8, 256, 3072], P(('groups', 'tm'), 'head'), parts along dimension 0, may hold values from -6 to 6
- residual: bfloat16 [8, 256, 5120], P(('groups', 'tm'), None, 'head'), parts along dimension 0, may hold values from -3 to 3
- fresh_frame: bfloat16 [512, 5120], P('groups', 'head'), parts along dimension 0, may hold values from -6 to 6
- out_weight: bfloat16 [3072, 5120], P('tm', 'head'), may hold values from -0.875 to 0.875
- time_weight: bfloat16 [256, 5120], P(None, 'head'), may hold values from -0.375 to 0.375
- noise_steps: int32 [8], P(('groups', 'tm')), parts along dimension 0, may hold values from 0 to 49, as said below
- frame_mask: int32 [8, 4], P(('groups', 'tm')), parts along dimension 0, may hold values from 0 to 1, as said below
Outputs:
- rolled: bfloat16 [8, 256, 5120], P(('groups', 'tm'), None, 'head'), parts along dimension 0
There are 2 independent parts, one for each index of `groups`. A program takes and returns all parts, laid end to end along the dimension named above; an argument that names none is the same for every part. Nothing has to cross between parts.
Inputs may be any that keep to these rules, and one draw needn't show every extreme that they name: frame_mask[i, j] is 1 exactly for i - L_i < j <= i, with a whole number L_i from 1 to 4 for each frame i; the last frame has L_i = 4. `noise_steps`: never falling along the frames; the first frame has 0 and the last 49.
All inputs are finite; a program needn't handle non-finite values.
Results may differ from a plain program's by a relative error of at most 0.0065.
Values may be sent and summed in bfloat16 or wider, within the bound.
A program may use at most 64 MiB of HBM per device.

v0:
```python
import math

import jax
import jax.numpy as jnp
from jax import lax
from jax.sharding import PartitionSpec as P

HD = 128
FREQ = 256
STEPS = 50


def shifted(value, axis, steps):
    count = lax.axis_size(axis)
    leading, last = (max(0, -steps), min(count, count - steps))
    return lax.ppermute(value, axis, [(source, source + steps) for source in range(leading, last)])


def time_features(noise_steps):
    timestep = 1000.0 * (noise_steps.astype(jnp.float32) + 1.0) / STEPS
    half = FREQ // 2
    rates = jnp.exp(-math.log(10000.0) * jnp.arange(half).astype(jnp.float32) / half)
    angles = timestep[:, None] * rates[None, :]
    return jnp.concatenate([jnp.cos(angles), jnp.sin(angles)], axis=1)


def on_device(
    queries, keys, values, residual, fresh_frame, out_weight, time_weight, noise_steps, frame_mask
):
    query_local, key_local, value_local = (
        lax.all_to_all(queries, "head", split_axis=2, concat_axis=1, tiled=True),
        lax.all_to_all(keys, "head", split_axis=2, concat_axis=1, tiled=True),
        lax.all_to_all(values, "head", split_axis=2, concat_axis=1, tiled=True),
    )
    tokens = query_local.shape[1]
    heads_here = query_local.shape[2] // HD
    scale = 1.0 / math.sqrt(HD)
    query_heads = query_local[0].reshape(tokens, heads_here, HD)
    key_value = jnp.stack([key_local[0], value_local[0]], axis=0)
    frame = lax.axis_index("tm")
    frames_total = lax.axis_size("tm")
    window = min(8, frames_total)
    mask_row = frame_mask[0]
    columns = jnp.arange(mask_row.shape[0], dtype=jnp.int32)

    def allowed_at(offset):
        hits = jnp.sum(jnp.where(columns == frame - offset, mask_row, 0))
        return hits > 0

    def absorb(state, block, allowed):
        running_max, weight_sum, accumulated = state
        key_heads = block[0].reshape(tokens, heads_here, HD)
        value_heads = block[1].reshape(tokens, heads_here, HD)
        scores = (
            jnp.einsum("qhd,khd->hqk", query_heads, key_heads, preferred_element_type=jnp.float32)
            * scale
        )
        new_max = jnp.where(allowed, jnp.maximum(running_max, jnp.max(scores, axis=2)), running_max)
        lifted = jnp.where(allowed, jnp.exp(jnp.minimum(scores - new_max[:, :, None], 0.0)), 0.0)
        factor = jnp.exp(running_max - new_max)
        weight_sum = weight_sum * factor + jnp.sum(lifted, axis=2)
        rounded = lifted.astype(jnp.bfloat16)
        accumulated = accumulated * jnp.transpose(factor)[:, :, None] + jnp.einsum(
            "hqk,khd->qhd", rounded, value_heads, preferred_element_type=jnp.float32
        )
        return (new_max, weight_sum, accumulated)

    state = (
        jnp.full((heads_here, tokens), -1e30, jnp.float32),
        jnp.zeros((heads_here, tokens), jnp.float32),
        jnp.zeros((tokens, heads_here, HD), jnp.float32),
    )
    state = absorb(state, key_value, allowed_at(0))
    moving = key_value
    for offset in range(1, window):
        moving = shifted(moving, "tm", 1)
        state = absorb(state, moving, allowed_at(offset))
    running_max, weight_sum, accumulated = state
    attention = (
        (accumulated / jnp.transpose(weight_sum)[:, :, None])
        .reshape(tokens, heads_here * HD)
        .astype(jnp.bfloat16)
    )
    weight_cols = lax.all_gather(out_weight, "tm", axis=0, tiled=True)
    projected = jnp.dot(
        lax.all_gather(attention, "head", axis=1, tiled=True),
        weight_cols,
        preferred_element_type=jnp.float32,
    )
    gate = jnp.dot(
        time_features(noise_steps), time_weight.astype(jnp.float32), precision=lax.Precision.HIGHEST
    )
    updated = (residual[0].astype(jnp.float32) + gate * projected).astype(jnp.bfloat16)
    moved = shifted(updated, "tm", -1)
    rolled = jnp.where(frame == frames_total - 1, fresh_frame, moved)
    return rolled[None]


def solution(mesh):
    placed = (
        P(("groups", "tm"), "head", None),
        P(("groups", "tm"), "head", None),
        P(("groups", "tm"), "head", None),
        P(("groups", "tm"), None, "head"),
        P("groups", "head"),
        P("tm", "head"),
        P(None, "head"),
        P(("groups", "tm")),
        P(("groups", "tm"), None),
    )
    return jax.shard_map(
        on_device,
        mesh=mesh,
        in_specs=placed,
        out_specs=P(("groups", "tm"), None, "head"),
        check_vma=False,
    )
```

profile of v0, /device:TPU:0, one launch (start us, length us, event | category | flops | bytes accessed | tf_op | source)
XLA Modules:
  0.0 350.7 jit_solution(9926861367071621732)
XLA Ops:
  6.5 3.6 %copy.96 = bf16[1,64,3072]{1,0,2:T(2,128)(2,1)S(1)} copy(bf16[1,64,3072]{2,1,0:T(8,128)(2,1)} %param.10) | data formatting | bytes 786432 | tf_op args[1]
  10.2 0.5 broadcast.158
  10.7 16.9 %reduce.3 = bf16[3072,64]{1,0:T(8,128)(2,1)S(1)} reduce(bf16[3072,1,64]{2,1,0:T(2,128)(2,1)S(1)} %bitcast.180, bf16[]{:T(256)} %broadcast.158), dimensions={1}, to_apply=%bitcast.157.reduce_sub_computation | reduce | bytes 786434
  27.6 1.3 reshape.82
  28.9 4.2 %all-to-all-start.1 = ((bf16[4,2,24576]{2,1,0:T(2,128)(2,1)}), bf16[4,2,24576]{2,1,0:T(2,128)(2,1)S(1)}, u32[]{:S(2)}, u32[]{:S(2)}) async-start(bf16[4,2,24576]{2,1,0:T(2,128)(2,1)} %reshape.82), calls=%async_computation.1 | async-start | bytes 786432 | tf_op jit(solution)/shard_map/all_to_all | solution.py:32
  33.1 3.6 %copy.102 = bf16[1,64,3072]{1,0,2:T(2,128)(2,1)S(1)} copy(bf16[1,64,3072]{2,1,0:T(8,128)(2,1)} %param.11) | data formatting | bytes 786432 | tf_op args[2]
  36.7 16.9 %reduce.2 = bf16[3072,64]{1,0:T(8,128)(2,1)S(1)} reduce(bf16[3072,1,64]{2,1,0:T(2,128)(2,1)S(1)} %bitcast.182, bf16[]{:T(256)} %broadcast.158), dimensions={1}, to_apply=%bitcast.155.reduce_sub_computation | reduce | bytes 786434
  53.6 1.3 reshape.80
  54.9 3.6 %all-to-all-start.2 = ((bf16[4,2,24576]{2,1,0:T(2,128)(2,1)}), bf16[4,2,24576]{2,1,0:T(2,128)(2,1)S(1)}, u32[]{:S(2)}, u32[]{:S(2)}) async-start(bf16[4,2,24576]{2,1,0:T(2,128)(2,1)} %reshape.80), calls=%async_computation.2 | async-start | bytes 786432 | tf_op jit(solution)/shard_map/all_to_all | solution.py:33
  58.5 0.8 reshape.83
  59.3 1.5 copy.97
  60.8 0.3 all_to_all.41
  61.2 4.8 %all-to-all-done.2 = bf16[4,2,24576]{2,1,0:T(2,128)(2,1)S(1)} async-done(((bf16[4,2,24576]{2,1,0:T(2,128)(2,1)}), bf16[4,2,24576]{2,1,0:T(2,128)(2,1)S(1)}, u32[]{:S(2)}, u32[]{:S(2)}) %all-to-all-start.2) | async-done | bytes 393248 | tf_op jit(solution)/shard_map/all_to_all | solution.py:33
  65.9 0.8 reshape.81
  66.7 1.5 copy.103
  68.3 0.3 all_to_all.44
  68.6 0.9 pad_maximum_fusion
  69.5 5.1 %collective-permute-start = (bf16[2,256,768]{2,1,0:T(8,128)(2,1)}, bf16[2,256,768]{2,1,0:T(8,128)(2,1)}, u32[]{:S(2)}, u32[]{:S(2)}) collective-permute-start(bf16[2,256,768]{2,1,0:T(8,128)(2,1)} %pad_maximum_fusion), channel_id=1, source_target_pairs={{0,4},{4,8},{8,12},{1,5},{5,9},{9,13},{2,6},{6,10},{10,14},{3,7},{... | collective-permute-start | bytes 2359304 | tf_op jit(solution)/shard_map/ppermute | solution.py:16
  74.6 1.8 copy.93
  76.4 17.8 %reduce.4 = bf16[3072,64]{1,0:T(8,128)(2,1)} reduce(bf16[3072,1,64]{2,1,0:T(2,128)(2,1)S(1)} %bitcast.181, bf16[]{:T(256)} %broadcast.158), dimensions={1}, to_apply=%bitcast.159.reduce_sub_computation | reduce | bytes 786434
  94.2 2.4 reshape.84
  96.7 3.5 all-to-all-start
  100.2 3.7 %collective-permute-start.1 = (bf16[2,256,768]{2,1,0:T(8,128)(2,1)}, bf16[2,256,768]{2,1,0:T(8,128)(2,1)}, u32[]{:S(2)}, u32[]{:S(2)}) collective-permute-start(bf16[2,256,768]{2,1,0:T(8,128)(2,1)} %collective-permute-done), channel_id=1, source_target_pairs={{0,4},{4,8},{8,12},{1,5},{5,9},{9,13},{2,6},{6,10},{10,14},{3,7},{... | collective-permute-start | bytes 2359304 | tf_op jit(solution)/shard_map/ppermute | solution.py:16
  103.9 0.8 fusion.61
  107.3 1.2 reshape_squeeze_stack_squeeze.6
  108.5 0.6 copy.131
  109.2 0.8 reshape.85
  110.0 1.5 copy.94
  111.5 0.3 all_to_all.38
  111.9 0.5 reshape_squeeze.21
  112.3 1.2 reshape.78
  113.6 2.1 fusion.74
  115.7 1.2 fusion.73
  116.9 0.2 copy.109
  117.0 0.9 copy.112
  118.0 2.8 collective-permute-done.1
  120.7 5.3 %collective-permute-start.2 = (bf16[2,256,768]{2,1,0:T(8,128)(2,1)}, bf16[2,256,768]{2,1,0:T(8,128)(2,1)}, u32[]{:S(2)}, u32[]{:S(2)}) collective-permute-start(bf16[2,256,768]{2,1,0:T(8,128)(2,1)} %collective-permute-done.1), channel_id=1, source_target_pairs={{0,4},{4,8},{8,12},{1,5},{5,9},{9,13},{2,6},{6,10},{10,14},{3,7},{... | collective-permute-start | bytes 2359304 | tf_op jit(solution)/shard_map/ppermute | solution.py:16
  126.0 0.4 bitcast_reduce_fusion.2
  126.4 1.9 fusion.72
  128.3 1.2 copy.114
  129.5 0.9 copy.117
  130.5 1.6 bitcast_reduce_fusion.1
  132.0 9.9 %collective-permute-done.2 = bf16[2,256,768]{2,1,0:T(8,128)(2,1)} collective-permute-done((bf16[2,256,768]{2,1,0:T(8,128)(2,1)}, bf16[2,256,768]{2,1,0:T(8,128)(2,1)}, u32[]{:S(2)}, u32[]{:S(2)}) %collective-permute-start.2) | collective-permute-done | bytes 786464 | tf_op jit(solution)/shard_map/ppermute | solution.py:16
  141.9 1.9 fusion.71
  143.8 1.2 copy.119
  145.0 2.2 bitcast_reduce_fusion
  147.2 0.2 copy.122
  147.3 0.7 maximum_select_fusion
  148.1 2.2 fusion.20
  150.4 0.6 fusion.24
  151.1 0.7 copy-done.2
  151.9 0.4 fusion.18
  152.4 0.4 fusion.12
  152.8 0.5 copy-done.6
  153.4 0.4 fusion.14
  153.8 1.2 fusion.19
  155.1 0.7 all-gather.5.cloned.1.call-update
  156.5 0.4 convolution_reduce_fusion
  156.9 18.9 %all-gather.3.cloned.1.call-done = bf16[256,3072]{0,1:T(8,128)(2,1)} async-done(((bf16[256,768]{0,1:T(8,128)(2,1)}), bf16[256,3072]{0,1:T(8,128)(2,1)}) %all-gather.3.cloned.1.call-update) | async-done | bytes 1572880 | tf_op jit(solution)/shard_map/all_gather | solution.py:86
  175.8 142.6 %all-gather.5.cloned.1.call-done = bf16[3072,1280]{1,0:T(8,128)(2,1)} async-done(((bf16[768,1280]{1,0:T(8,128)(2,1)}), bf16[3072,1280]{1,0:T(8,128)(2,1)}) %all-gather.5.cloned.1.call-update) | async-done | bytes 7864336 | tf_op jit(solution)/shard_map/all_gather | solution.py:84
  318.5 6.0 %fusion.1 = bf16[256,1280]{1,0:T(8,128)(2,1)S(1)} fusion(bf16[256,3072]{0,1:T(8,128)(2,1)} %all-gather.3.cloned.1.call-done, bf16[3072,1280]{1,0:T(8,128)(2,1)} %all-gather.5.cloned.1.call-done, bf16[1,256,1280]{2,1,0:T(8,128)(2,1)S(1)} %copy-done.8, f32[1280]{0:T(1024)S(1)} %convolution_reduce_fusion), kind=kOutput, calls=%fused_computation.2 | convolution fusion | flops 2014576640 | bytes 10753024 | tf_op jit(solution)/shard_map/dot_general | solution.py:85
  324.4 1.3 collective-permute-start.3
  325.7 17.2 %collective-permute-done.3 = bf16[256,1280]{1,0:T(8,128)(2,1)S(1)} collective-permute-done((bf16[256,1280]{1,0:T(8,128)(2,1)S(1)}, bf16[256,1280]{1,0:T(8,128)(2,1)S(1)}, u32[]{:S(2)}, u32[]{:S(2)}) %collective-permute-start.3) | collective-permute-done | bytes 655392 | tf_op jit(solution)/shard_map/ppermute | solution.py:16
  343.0 0.9 select_bitcast_fusion
  (35 shorter events, 0.6 us)
Async XLA Ops:
  6.5 149.9 %copy-start = (bf16[256,1280]{1,0:T(8,128)(2,1)S(1)}, bf16[256,1280]{1,0:T(8,128)(2,1)}, u32[]{:S(2)}) copy-start(bf16[256,1280]{1,0:T(8,128)(2,1)} %param.15) | copy-start | bytes 1966084
  28.9 26.0 %all-to-all-start.1 = ((bf16[4,2,24576]{2,1,0:T(2,128)(2,1)}), bf16[4,2,24576]{2,1,0:T(2,128)(2,1)S(1)}, u32[]{:S(2)}, u32[]{:S(2)}) async-start(bf16[4,2,24576]{2,1,0:T(2,128)(2,1)} %reshape.82), calls=%async_computation.1 | async-start | bytes 786432 | tf_op jit(solution)/shard_map/all_to_all | solution.py:32
  54.9 11.1 %all-to-all-start.2 = ((bf16[4,2,24576]{2,1,0:T(2,128)(2,1)}), bf16[4,2,24576]{2,1,0:T(2,128)(2,1)S(1)}, u32[]{:S(2)}, u32[]{:S(2)}) async-start(bf16[4,2,24576]{2,1,0:T(2,128)(2,1)} %reshape.80), calls=%async_computation.2 | async-start | bytes 786432 | tf_op jit(solution)/shard_map/all_to_all | solution.py:33
  68.2 6.3 %copy-start.10 = (bf16[1,64,3072]{2,1,0:T(8,128)(2,1)S(1)}, bf16[1,64,3072]{2,1,0:T(8,128)(2,1)}, u32[]{:S(2)}) copy-start(bf16[1,64,3072]{2,1,0:T(8,128)(2,1)} %param.9) | copy-start | bytes 1179652
  69.5 30.7 %collective-permute-start = (bf16[2,256,768]{2,1,0:T(8,128)(2,1)}, bf16[2,256,768]{2,1,0:T(8,128)(2,1)}, u32[]{:S(2)}, u32[]{:S(2)}) collective-permute-start(bf16[2,256,768]{2,1,0:T(8,128)(2,1)} %pad_maximum_fusion), channel_id=1, source_target_pairs={{0,4},{4,8},{8,12},{1,5},{5,9},{9,13},{2,6},{6,10},{10,14},{3,7},{... | collective-permute-start | bytes 2359304 | tf_op jit(solution)/shard_map/ppermute | solution.py:16
  94.2 9.7 %copy-start.12 = (s32[1,4]{1,0:T(1,128)S(1)}, s32[1,4]{1,0:T(1,128)}, u32[]{:S(2)}) copy-start(s32[1,4]{1,0:T(1,128)} %param.17) | copy-start | bytes 52
  96.7 12.5 %all-to-all-start = ((bf16[4,2,24576]{2,1,0:T(2,128)(2,1)}), bf16[4,2,24576]{2,1,0:T(2,128)(2,1)S(1)}, u32[]{:S(2)}, u32[]{:S(2)}) async-start(bf16[4,2,24576]{2,1,0:T(2,128)(2,1)} %reshape.84), calls=%async_computation | async-start | bytes 786432 | tf_op jit(solution)/shard_map/all_to_all | solution.py:31
  100.1 75.7 %all-gather.3.cloned.1.call-start = ((), (), s32[]{:S(2)}) async-start(), calls=%async_computation.3 | async-start | bytes 1966080 | tf_op jit(solution)/shard_map/all_gather | solution.py:86
  100.2 20.5 %collective-permute-start.1 = (bf16[2,256,768]{2,1,0:T(8,128)(2,1)}, bf16[2,256,768]{2,1,0:T(8,128)(2,1)}, u32[]{:S(2)}, u32[]{:S(2)}) collective-permute-start(bf16[2,256,768]{2,1,0:T(8,128)(2,1)} %collective-permute-done), channel_id=1, source_target_pairs={{0,4},{4,8},{8,12},{1,5},{5,9},{9,13},{2,6},{6,10},{10,14},{3,7},{... | collective-permute-start | bytes 2359304 | tf_op jit(solution)/shard_map/ppermute | solution.py:16
  111.8 1.8 copy-start.4
  120.7 21.2 %collective-permute-start.2 = (bf16[2,256,768]{2,1,0:T(8,128)(2,1)}, bf16[2,256,768]{2,1,0:T(8,128)(2,1)}, u32[]{:S(2)}, u32[]{:S(2)}) collective-permute-start(bf16[2,256,768]{2,1,0:T(8,128)(2,1)} %collective-permute-done.1), channel_id=1, source_target_pairs={{0,4},{4,8},{8,12},{1,5},{5,9},{9,13},{2,6},{6,10},{10,14},{3,7},{... | collective-permute-start | bytes 2359304 | tf_op jit(solution)/shard_map/ppermute | solution.py:16
  148.1 2.2 copy-start.1
  148.1 2.3 copy-start.3
  150.4 0.7 copy-start.11
  150.4 1.4 copy-start.2
  150.4 1.5 copy-start.9
  151.1 1.3 copy-start.5
  152.4 1.0 copy-start.6
  155.0 163.5 %copy-start.8 = (bf16[1,256,1280]{2,1,0:T(8,128)(2,1)S(1)}, bf16[1,256,1280]{2,1,0:T(8,128)(2,1)}, u32[]{:S(2)}) copy-start(bf16[1,256,1280]{2,1,0:T(8,128)(2,1)} %param.12) | copy-start | bytes 1966084
  155.0 163.4 %all-gather.5.cloned.1.call-start = ((), (), s32[]{:S(2)}) async-start(), calls=%async_computation.4 | async-start | bytes 9830400 | tf_op jit(solution)/shard_map/all_gather | solution.py:84
  156.9 186.1 %copy-start.7 = (bf16[256,1280]{1,0:T(8,128)(2,1)S(1)}, bf16[256,1280]{1,0:T(8,128)(2,1)}, u32[]{:S(2)}) copy-start(bf16[256,1280]{1,0:T(8,128)(2,1)} %param.13) | copy-start | bytes 1966084
  324.4 18.5 %collective-permute-start.3 = (bf16[256,1280]{1,0:T(8,128)(2,1)S(1)}, bf16[256,1280]{1,0:T(8,128)(2,1)S(1)}, u32[]{:S(2)}, u32[]{:S(2)}) collective-permute-start(bf16[256,1280]{1,0:T(8,128)(2,1)S(1)} %fusion.1), channel_id=1, source_target_pairs={{4,0},{8,4},{12,8},{5,1},{9,5},{13,9},{6,2},{10,6},{14,10},{7,3},{... | collective-permute-start | bytes 1966088 | tf_op jit(solution)/shard_map/ppermute | solution.py:16
Sparse Core Ops, SparseCore 0:
  155.1 20.6 all-gather.2
  177.4 141.0 all-gather.4
where the time goes:
time: 352 us; the launch traced here: 351 us
  waiting for transfers between devices  197 us (56%)
  other arithmetic  57.8 us (16%)
  local copies, waits for them, and re-layouts  37.1 us (11%)
  starting transfers between devices  26.8 us (8%)
  between operations  17 us (5%)
  matrix products  15.1 us (4%)
    all_gather x1, waiting for transfers between devices, on_device(): weight_cols = lax.all_gather(out_weight, 'tm', axis=0, tiled=True)  143 us
    unnamed x3, other arithmetic  51.6 us
    ppermute x4, waiting for transfers between devices, shifted(): lax.ppermute(value, axis, [(source, source + steps) for source in range(l...  29.9 us
    all_gather x1, waiting for transfers between devices, on_device(): lax.all_gather(attention, 'head', axis=1, tiled=True)  18.9 us
    unnamed x36, local copies, waits for them, and re-layouts  18.5 us
    ppermute x4, starting transfers between devices, shifted(): lax.ppermute(value, axis, [(source, source + steps) for source in range(l...  15.3 us
  transfers between devices with their start and end apart: 9, of which 6 were waited for; matrix products, arithmetic and copies ran while one was open for 18% of the time, Pallas kernels for 0%

commit v1 on v0

--- a/solution.py
+++ b/solution.py
@@ -1,8 +1,11 @@
+import functools
 import math
 
 import jax
 import jax.numpy as jnp
 from jax import lax
+from jax.experimental import pallas as pl
+from jax.experimental.pallas import tpu as pltpu
 from jax.sharding import PartitionSpec as P
 
 HD = 128
@@ -96,6 +99,382 @@
     return rolled[None]
 
 
+def fused_kernel(
+    T, G, C, hp, pieces,
+    q_ref, k_ref, v_ref, res_ref, fresh_ref, w_ref, meta_ref,
+    out_ref,
+    qb, kb, vb, ab, mb, wb, rb, pb, down_out, down_in, up_out, up_in,
+    load_sem, meta_send, meta_recv, qkv_send, qkv_recv, pass_send, pass_recv,
+    ax_send, ax_recv, ac_send, ac_recv, dn_send, dn_recv, up_send, up_recv,
+):
+    t = lax.axis_index("tm")
+    h = lax.axis_index("head")
+    x = h // C
+    c = lax.rem(h, C)
+    H = G * C
+    tl = q_ref.shape[1]
+    cw = hp * HD
+    tokens = tl * H
+    half = G * tl
+    nb = w_ref.shape[1] // pieces
+    gate_rows = w_ref.shape[1] // HD
+
+    def to(tt, hh):
+        return dict(device_id={"tm": tt, "head": hh}, device_id_type=pl.DeviceIdType.MESH)
+
+    def landed(ref, sem):
+        pltpu.make_async_copy(ref, ref, sem).wait()
+
+    others = [(dt, dx) for dt in range(T) for dx in reversed(range(G)) if (dt, dx) != (0, 0)]
+
+    loads = [
+        pltpu.make_async_copy(w_ref, wb, load_sem.at[0]),
+        pltpu.make_async_copy(res_ref.at[0], rb, load_sem.at[1]),
+    ]
+    for copy in loads:
+        copy.start()
+
+    barrier = pltpu.get_barrier_semaphore()
+    for dt, dx in others:
+        pl.semaphore_signal(
+            barrier, inc=1, **to(lax.rem(t + dt, T), lax.rem(x + dx, G) * C + c)
+        )
+    for dc in range(1, C):
+        pl.semaphore_signal(barrier, inc=1, **to(t, x * C + lax.rem(c + dc, C)))
+    pl.semaphore_wait(barrier, len(others) + C - 1)
+
+    own_meta = pltpu.make_async_copy(meta_ref, mb.at[t], meta_recv.at[t])
+    own_meta.start()
+    meta_copies = []
+    for dt in range(1, T):
+        meta_copies.append(
+            pltpu.make_async_remote_copy(
+                src_ref=meta_ref, dst_ref=mb.at[t], send_sem=meta_send.at[dt],
+                recv_sem=meta_recv.at[t], **to(lax.rem(t + dt, T), h),
+            )
+        )
+        meta_copies[-1].start()
+
+    sources = ((q_ref, qb), (k_ref, kb), (v_ref, vb))
+
+    def slot(kind, f, xs):
+        return qb.at[f, xs] if kind == 0 else sources[kind][1].at[f, xs * C + c]
+
+    def block(kind, tt, xx):
+        column = pl.multiple_of((tt * G + xx) * cw, HD)
+        return sources[kind][0].at[0, :, pl.ds(column, cw)]
+
+    def outgoing(kind, dt, dx):
+        tt, xx = lax.rem(t + dt, T), lax.rem(x + dx, G)
+        return pltpu.make_async_remote_copy(
+            src_ref=block(kind, tt, xx), dst_ref=slot(kind, t, x),
+            send_sem=qkv_send.at[kind, dt, dx], recv_sem=qkv_recv.at[kind, t, x],
+            **to(tt, xx * C + c),
+        )
+
+    def own(kind):
+        return pltpu.make_async_copy(block(kind, t, x), slot(kind, t, x), qkv_recv.at[kind, t, x])
+
+    for dt, dx in others:
+        for kind in (1, 2):
+            outgoing(kind, dt, dx).start()
+
+        @pl.when(t > 0)
+        def _():
+            outgoing(0, dt, dx).start()
+
+    for kind in (1, 2):
+        own(kind).start()
+
+    @pl.when(t > 0)
+    def _():
+        own(0).start()
+
+    def passed(kind, dc, f, xs):
+        return pltpu.make_async_remote_copy(
+            src_ref=slot(kind, f, xs), dst_ref=slot(kind, f, xs),
+            send_sem=pass_send.at[kind - 1, dc, f, xs], recv_sem=pass_recv.at[kind - 1, dc, f, xs],
+            **to(t, x * C + lax.rem(c + dc, C)),
+        )
+
+    for dt in range(T):
+        for dx in range(G):
+            f, xs = lax.rem(t + dt, T), lax.rem(x + dx, G)
+            for kind in (1, 2):
+                landed(slot(kind, f, xs), qkv_recv.at[kind, f, xs])
+                for dc in range(1, C):
+                    passed(kind, dc, f, xs).start()
+    for f in range(T):
+        for xs in range(G):
+            if f > 0:
+                landed(slot(0, f, xs), qkv_recv.at[0, f, xs])
+            for kind in (1, 2):
+                for dc in range(1, C):
+                    from_c = xs * C + lax.rem(c + C - dc, C)
+                    landed(sources[kind][1].at[f, from_c], pass_recv.at[kind - 1, dc, f, xs])
+        landed(mb.at[f], meta_recv.at[f])
+    for copy in loads:
+        copy.wait()
+
+    def across(r, dx):
+        xx = lax.rem(x + dx, G)
+        return pltpu.make_async_remote_copy(
+            src_ref=ab.at[x, r, c], dst_ref=ab.at[x, r, c],
+            send_sem=ax_send.at[r, dx], recv_sem=ax_recv.at[r, dx],
+            **to(t, xx * C + c),
+        )
+
+    def aside(r, dx, dc):
+        xs = lax.rem(x + dx, G)
+        return pltpu.make_async_remote_copy(
+            src_ref=ab.at[xs, r, c], dst_ref=ab.at[xs, r, c],
+            send_sem=ac_send.at[r, dx, dc], recv_sem=ac_recv.at[r, dx, dc],
+            **to(t, x * C + lax.rem(c + dc, C)),
+        )
+
+    scale = 1.0 / math.sqrt(HD)
+    for r in range(T - 1):
+        f = r + 1
+        keys_here = (f + 1) * tokens
+        allowed = jnp.concatenate(
+            [
+                jnp.broadcast_to(mb[f, gate_rows + g : gate_rows + g + 1, 0:1], (1, tokens))
+                for g in range(f + 1)
+            ],
+            axis=1,
+        )
+        for j in range(hp):
+            cols = slice(j * HD, (j + 1) * HD)
+            query = qb[f, :, :, cols].reshape(half, HD)
+            key = kb[0 : f + 1, :, :, cols].reshape(keys_here, HD)
+            value = vb[0 : f + 1, :, :, cols].reshape(keys_here, HD)
+            scores = (
+                lax.dot_general(
+                    query, key, (((1,), (1,)), ((), ())), preferred_element_type=jnp.float32
+                )
+                * scale
+            )
+            scores = jnp.where(allowed > 0.5, scores, -1e30)
+            peak = jnp.max(scores, axis=1, keepdims=True)
+            lifted = jnp.exp(scores - peak)
+            total = jnp.sum(lifted, axis=1, keepdims=True)
+            mixed = jnp.dot(
+                lifted.astype(jnp.bfloat16), value, preferred_element_type=jnp.float32
+            )
+            ab[x, r, c, :, cols] = (mixed / total).astype(jnp.bfloat16)
+        for dx in range(1, G):
+            across(r, dx).start()
+        for dc in range(1, C):
+            aside(r, 0, dc).start()
+
+    def down(r, p):
+        return pltpu.make_async_remote_copy(
+            src_ref=down_out.at[r, p], dst_ref=down_in.at[r, p],
+            send_sem=dn_send.at[r, p], recv_sem=dn_recv.at[r, p], **to(t - 1, h),
+        )
+
+    def up(r, p):
+        return pltpu.make_async_remote_copy(
+            src_ref=up_out.at[r, p], dst_ref=up_in.at[r, p],
+            send_sem=up_send.at[r, p], recv_sem=up_recv.at[r, p], **to(t + 1, h),
+        )
+
+    for r in range(T - 1):
+        for dx in range(1, G):
+            xs = lax.rem(x + G - dx, G)
+            landed(ab.at[xs, r, c], ax_recv.at[r, dx])
+            for dc in range(1, C):
+                aside(r, G - dx, dc).start()
+        for dx in range(G):
+            for dc in range(1, C):
+                xs, cs = lax.rem(x + dx, G), lax.rem(c + C - dc, C)
+                landed(ab.at[xs, r, cs], ac_recv.at[r, dx, dc])
+        for p in range(pieces):
+            cols = slice(p * nb, (p + 1) * nb)
+            gate = jnp.concatenate(
+                [mb[r + 1, b : b + 1, :] for b in range(p * nb // HD, (p + 1) * nb // HD)], axis=1
+            )
+            partial = 0.0
+            for xs in range(G):
+                partial += jnp.dot(
+                    ab[xs, r].reshape(tokens, cw),
+                    wb[xs * cw : (xs + 1) * cw, cols],
+                    preferred_element_type=jnp.float32,
+                )
+            pb[r, p] = partial * gate
+
+            @pl.when(t == r + 1)
+            def _():
+                for cs in range(C):
+                    for xs in range(G):
+                        rows = (cs * G + xs) * tl
+                        token = (xs * C + cs) * tl
+                        pb[r, p, rows : rows + tl, :] += rb[token : token + tl, cols].astype(
+                            jnp.float32
+                        )
+
+            @pl.when(t == T - 1)
+            def _():
+                down_out[r, p] = pb[r, p].astype(jnp.bfloat16)
+                down(r, p).start()
+
+            if r > 0:
+
+                @pl.when(t == 0)
+                def _():
+                    up_out[r, p] = pb[r, p].astype(jnp.bfloat16)
+                    up(r, p).start()
+
+    for r in reversed(range(2, T - 1)):
+        for p in range(pieces):
+
+            @pl.when((t > 0) & (t < r))
+            def _():
+                landed(up_in.at[r, p], up_recv.at[r, p])
+                up_out[r, p] = (pb[r, p] + up_in[r, p].astype(jnp.float32)).astype(jnp.bfloat16)
+                up(r, p).start()
+
+    for r in range(T - 2):
+        for p in range(pieces):
+
+            @pl.when((t > r) & (t < T - 1))
+            def _():
+                landed(down_in.at[r, p], dn_recv.at[r, p])
+                down_out[r, p] = (pb[r, p] + down_in[r, p].astype(jnp.float32)).astype(
+                    jnp.bfloat16
+                )
+                down(r, p).start()
+
+    for r in range(T - 1):
+
+        @pl.when(t == r)
+        def _():
+            for p in range(pieces):
+                cols = slice(p * nb, (p + 1) * nb)
+                landed(down_in.at[r, p], dn_recv.at[r, p])
+                if r > 0:
+                    landed(up_in.at[r, p], up_recv.at[r, p])
+                for cs in range(C):
+                    for xs in range(G):
+                        rows = slice((cs * G + xs) * tl, (cs * G + xs + 1) * tl)
+                        token = (xs * C + cs) * tl
+                        total = pb[r, p, rows, :] + down_in[r, p, rows, :].astype(jnp.float32)
+                        if r > 0:
+                            total += up_in[r, p, rows, :].astype(jnp.float32)
+                        out_ref[token : token + tl, cols] = total.astype(out_ref.dtype)
+
+    @pl.when(t == T - 1)
+    def _():
+        copy = pltpu.make_async_copy(fresh_ref, out_ref, load_sem.at[2])
+        copy.start()
+        copy.wait()
+
+    for copy in meta_copies:
+        copy.wait_send()
+    for dt, dx in others:
+        for kind in (1, 2):
+            outgoing(kind, dt, dx).wait_send()
+
+        @pl.when(t > 0)
+        def _():
+            outgoing(0, dt, dx).wait_send()
+
+    for dc in range(1, C):
+        for f in range(T):
+            for xs in range(G):
+                for kind in (1, 2):
+                    passed(kind, dc, f, xs).wait_send()
+    for r in range(T - 1):
+        for dx in range(1, G):
+            across(r, dx).wait_send()
+        for dx in range(G):
+            for dc in range(1, C):
+                aside(r, dx, dc).wait_send()
+        for p in range(pieces):
+
+            @pl.when(t > r)
+            def _():
+                down(r, p).wait_send()
+
+            @pl.when(t < r)
+            def _():
+                up(r, p).wait_send()
+
+
+def fused(T, H, heads):
+    def on_device_fused(
+        queries, keys, values, residual, fresh_frame, out_weight, time_weight, noise_steps, frame_mask
+    ):
+        level_heads = heads // T
+        G = math.gcd(level_heads, H)
+        C = H // G
+        hp = level_heads // G
+        tl = queries.shape[1]
+        tokens = tl * H
+        width = out_weight.shape[1]
+        pieces = 2
+        nb = width // pieces
+        gate = jnp.dot(
+            time_features(noise_steps), time_weight.astype(jnp.float32), precision=lax.Precision.HIGHEST
+        )
+        gate_rows = width // HD
+        meta_rows = -(-(gate_rows + T) // 8) * 8
+        mask_rows = jnp.broadcast_to(frame_mask[0].astype(jnp.float32)[:, None], (T, HD))
+        meta = jnp.concatenate(
+            [
+                gate.reshape(gate_rows, HD),
+                mask_rows,
+                jnp.zeros((meta_rows - gate_rows - T, HD), jnp.float32),
+            ],
+            axis=0,
+        )
+        cw = hp * HD
+        bf16, f32 = jnp.bfloat16, jnp.float32
+        dma = pltpu.SemaphoreType.DMA
+        chunk = (T - 1, pieces, tokens, nb)
+        out = pl.pallas_call(
+            functools.partial(fused_kernel, T, G, C, hp, pieces),
+            out_shape=jax.ShapeDtypeStruct((tokens, width), bf16),
+            in_specs=[pl.BlockSpec(memory_space=pl.ANY)] * 7,
+            out_specs=pl.BlockSpec(memory_space=pltpu.VMEM),
+            scratch_shapes=[
+                pltpu.VMEM((T, G, tl, cw), bf16),
+                pltpu.VMEM((T, H, tl, cw), bf16),
+                pltpu.VMEM((T, H, tl, cw), bf16),
+                pltpu.VMEM((G, T - 1, C, G * tl, cw), bf16),
+                pltpu.VMEM((T, meta_rows, HD), f32),
+                pltpu.VMEM(out_weight.shape, bf16),
+                pltpu.VMEM((tokens, width), bf16),
+                pltpu.VMEM(chunk, f32),
+                pltpu.VMEM(chunk, bf16),
+                pltpu.VMEM(chunk, bf16),
+                pltpu.VMEM(chunk, bf16),
+                pltpu.VMEM(chunk, bf16),
+                dma((3,)),
+                dma((T,)),
+                dma((T,)),
+                dma((3, T, G)),
+                dma((3, T, G)),
+                dma((2, C, T, G)),
+                dma((2, C, T, G)),
+                dma((T - 1, G)),
+                dma((T - 1, G)),
+                dma((T - 1, G, C)),
+                dma((T - 1, G, C)),
+                dma((T - 1, pieces)),
+                dma((T - 1, pieces)),
+                dma((T - 1, pieces)),
+                dma((T - 1, pieces)),
+            ],
+            compiler_params=pltpu.CompilerParams(
+                collective_id=0, has_side_effects=True, vmem_limit_bytes=56 * 1024 * 1024
+            ),
+        )(queries, keys, values, residual, fresh_frame, out_weight, meta)
+        return out[None]
+
+    return on_device_fused
+
+
 def solution(mesh):
     placed = (
         P(("groups", "tm"), "head", None),
@@ -108,10 +487,16 @@
         P(("groups", "tm")),
         P(("groups", "tm"), None),
     )
-    return jax.shard_map(
-        on_device,
-        mesh=mesh,
-        in_specs=placed,
-        out_specs=P(("groups", "tm"), None, "head"),
-        check_vma=False,
-    )
+    def whole(*args):
+        frames, spread = mesh.shape["tm"], mesh.shape["head"]
+        heads = args[0].shape[2] // HD
+        fits = 1 < frames <= 4 and heads % frames == 0 and args[5].shape[1] % (spread * 2 * HD) == 0
+        return jax.shard_map(
+            fused(frames, spread, heads) if fits else on_device,
+            mesh=mesh,
+            in_specs=placed,
+            out_specs=P(("groups", "tm"), None, "head"),
+            check_vma=False,
+        )(*args)
+
+    return whole

time: 352 us -> 91.1 us (0.26)
  waiting for transfers between devices: 197 us -> 0 us
  Pallas kernels: 0 us -> 84.7 us
  other arithmetic: 57.8 us -> 1.4 us
  local copies, waits for them, and re-layouts: 37.1 us -> 3.45 us
  starting transfers between devices: 26.8 us -> 0 us
  between operations: 17 us -> 0.67 us
  matrix products: 15.1 us -> 0.63 us
    all_gather x2 -> x0, waiting for transfers between devices: 162 us -> none  [the longest x1 143 us: on_device(): weight_cols = lax.all_gather(out_weight, 'tm', axis=0, tiled=True)]
    pallas_call x0 -> x1, Pallas kernels: none -> 84.7 us  [on_device_fused(): pl.pallas_call(functools.partial(fused_kernel, T, G, C, hp, pieces), out_...]
    unnamed x3 -> x0, other arithmetic: 51.6 us -> none
    ppermute x4 -> x0, waiting for transfers between devices: 29.9 us -> none  [shifted(): lax.ppermute(value, axis, [(source, source + steps) for source in range(l...]
    ppermute x4 -> x0, starting transfers between devices: 15.3 us -> none  [shifted(): lax.ppermute(value, axis, [(source, source + steps) for source in range(l...]
    unnamed x36 -> x2, local copies, waits for them, and re-layouts: 18.5 us -> 3.29 us
    dot_general x10 -> x1, matrix products: 15.1 us -> 0.63 us  [on_device_fused(): jnp.dot(time_features(noise_steps), time_weight.astype(jnp.float32), prec...]
    all_to_all x3 -> x0, starting transfers between devices: 11.3 us -> none  [the longest x1 4.24 us: on_device(): lax.all_to_all(keys, 'head', split_axis=2, concat_axis=1, tiled=True)]
  transfers between devices with their start and end apart: 9 -> 0, of which waited for: 6 -> 0; matrix products, arithmetic and copies ran while one was open for 18% -> 0% of each run, Pallas kernels for 0% -> 0%
where the time goes in v1:
time: 91.1 us; the launch traced here: 90.9 us
  Pallas kernels  84.7 us (93%)
  local copies, waits for them, and re-layouts  3.45 us (4%)
  other arithmetic  1.4 us (2%)
    pallas_call x1, Pallas kernels, on_device_fused(): pl.pallas_call(functools.partial(fused_kernel, T, G, C, hp, pieces), out_...  84.7 us
    unnamed x2, local copies, waits for them, and re-layouts  3.29 us

profile of v1, /device:TPU:0, one launch (start us, length us, event | category | flops | bytes accessed | tf_op | source)
XLA Modules:
  0.0 90.9 jit_solution(11423449187492305757)
XLA Ops:
  0.7 0.7 convert_bitcast_fusion
  1.3 0.1 pad.1.clone
  1.4 0.1 pad.2.clone
  1.5 1.3 %copy.10 = bf16[256,1280]{0,1:T(8,128)(2,1)S(1)} copy(bf16[256,1280]{1,0:T(8,128)(2,1)} %param.15) | data formatting | bytes 1310720 | tf_op args[6]
  2.9 0.6 fusion
  3.5 0.7 maximum_maximum_fusion.meta_ref
  4.2 84.7 %shard_map.91 = bf16[256,1280]{1,0:T(8,128)(2,1)} custom-call(bf16[1,64,3072]{2,1,0:T(8,128)(2,1)} %q_ref.1, bf16[1,64,3072]{2,1,0:T(8,128)(2,1)} %k_ref.1, bf16[1,64,3072]{2,1,0:T(8,128)(2,1)} %v_ref.1, bf16[1,256,1280]{2,1,0:T(8,128)(2,1)} %res_ref.1, bf16[256,1280]{1,0:T(8,128)(2,1)} %fresh_ref.1, bf16[768,1280]{1,0:T(8,128)(2,1)} %w_ref.1, ...), custom_call_target="tpu_custom_call" | custom-call | tf_op jit(solution)/shard_map/pallas_call | solution.py:435
  88.9 2.0 %copy.16 = bf16[1,256,1280]{2,1,0:T(8,128)(2,1)} copy(bf16[1,256,1280]{2,1,0:T(8,128)(2,1)} %bitcast.16) | data formatting | bytes 1310720
  (3 shorter events, 0.1 us)

commit v2 on v1

--- a/solution.py
+++ b/solution.py
@@ -101,9 +101,9 @@
 
 def fused_kernel(
     T, G, C, hp, pieces,
-    q_ref, k_ref, v_ref, res_ref, fresh_ref, w_ref, meta_ref,
+    q_ref, k_ref, v_ref, res_ref, fresh_ref, w_ref, tw_ref, meta_ref,
     out_ref,
-    qb, kb, vb, ab, mb, wb, rb, pb, down_out, down_in, up_out, up_in,
+    qb, kb, vb, ab, mb, fb, gb, wb, twb, rb, pb, down_out, down_in, up_out, up_in,
     load_sem, meta_send, meta_recv, qkv_send, qkv_recv, pass_send, pass_recv,
     ax_send, ax_recv, ac_send, ac_recv, dn_send, dn_recv, up_send, up_recv,
 ):
@@ -117,7 +117,7 @@
     tokens = tl * H
     half = G * tl
     nb = w_ref.shape[1] // pieces
-    gate_rows = w_ref.shape[1] // HD
+    mask_row = FREQ // HD
 
     def to(tt, hh):
         return dict(device_id={"tm": tt, "head": hh}, device_id_type=pl.DeviceIdType.MESH)
@@ -130,6 +130,7 @@
     loads = [
         pltpu.make_async_copy(w_ref, wb, load_sem.at[0]),
         pltpu.make_async_copy(res_ref.at[0], rb, load_sem.at[1]),
+        pltpu.make_async_copy(tw_ref, twb, load_sem.at[2]),
     ]
     for copy in loads:
         copy.start()
@@ -164,25 +165,30 @@
         column = pl.multiple_of((tt * G + xx) * cw, HD)
         return sources[kind][0].at[0, :, pl.ds(column, cw)]
 
-    def outgoing(kind, dt, dx):
-        tt, xx = lax.rem(t + dt, T), lax.rem(x + dx, G)
+    def outgoing(kind, tt, dx):
+        xx = lax.rem(x + dx, G)
         return pltpu.make_async_remote_copy(
             src_ref=block(kind, tt, xx), dst_ref=slot(kind, t, x),
-            send_sem=qkv_send.at[kind, dt, dx], recv_sem=qkv_recv.at[kind, t, x],
+            send_sem=qkv_send.at[kind, tt, dx], recv_sem=qkv_recv.at[kind, t, x],
             **to(tt, xx * C + c),
         )
 
     def own(kind):
         return pltpu.make_async_copy(block(kind, t, x), slot(kind, t, x), qkv_recv.at[kind, t, x])
 
-    for dt, dx in others:
-        for kind in (1, 2):
-            outgoing(kind, dt, dx).start()
-
-        @pl.when(t > 0)
-        def _():
-            outgoing(0, dt, dx).start()
-
+    def each_outgoing(act):
+        for tt in reversed(range(T)):
+            for dx in reversed(range(G)):
+                for kind in (1, 2, 0):
+                    wanted = t > 0 if kind == 0 else t >= 0
+                    if dx == 0:
+                        wanted = wanted & (t != tt)
+
+                    @pl.when(wanted)
+                    def _():
+                        act(outgoing(kind, tt, dx))
+
+    each_outgoing(lambda copy: copy.start())
     for kind in (1, 2):
         own(kind).start()
 
@@ -197,14 +203,25 @@
             **to(t, x * C + lax.rem(c + dc, C)),
         )
 
-    for dt in range(T):
+    for copy in loads:
+        copy.wait()
+    fb[...] = jnp.zeros_like(fb)
+    for f in range(T):
+        landed(mb.at[f], meta_recv.at[f])
+        for b in range(mask_row):
+            fb[f : f + 1, b * HD : (b + 1) * HD] = mb[f, b : b + 1, :]
+    gb[...] = jnp.dot(
+        fb[...], twb[...].astype(jnp.float32),
+        precision=lax.Precision.HIGHEST, preferred_element_type=jnp.float32,
+    )
+
+    def arrive(f):
         for dx in range(G):
-            f, xs = lax.rem(t + dt, T), lax.rem(x + dx, G)
+            xs = lax.rem(x + dx, G)
             for kind in (1, 2):
                 landed(slot(kind, f, xs), qkv_recv.at[kind, f, xs])
                 for dc in range(1, C):
                     passed(kind, dc, f, xs).start()
-    for f in range(T):
         for xs in range(G):
             if f > 0:
                 landed(slot(0, f, xs), qkv_recv.at[0, f, xs])
@@ -212,9 +229,6 @@
                 for dc in range(1, C):
                     from_c = xs * C + lax.rem(c + C - dc, C)
                     landed(sources[kind][1].at[f, from_c], pass_recv.at[kind - 1, dc, f, xs])
-        landed(mb.at[f], meta_recv.at[f])
-    for copy in loads:
-        copy.wait()
 
     def across(r, dx):
         xx = lax.rem(x + dx, G)
@@ -233,12 +247,13 @@
         )
 
     scale = 1.0 / math.sqrt(HD)
-    for r in range(T - 1):
+
+    def attend(r):
         f = r + 1
         keys_here = (f + 1) * tokens
         allowed = jnp.concatenate(
             [
-                jnp.broadcast_to(mb[f, gate_rows + g : gate_rows + g + 1, 0:1], (1, tokens))
+                jnp.broadcast_to(mb[f, mask_row + g : mask_row + g + 1, 0:1], (1, tokens))
                 for g in range(f + 1)
             ],
             axis=1,
@@ -279,7 +294,7 @@
             send_sem=up_send.at[r, p], recv_sem=up_recv.at[r, p], **to(t + 1, h),
         )
 
-    for r in range(T - 1):
+    def project(r):
         for dx in range(1, G):
             xs = lax.rem(x + G - dx, G)
             landed(ab.at[xs, r, c], ax_recv.at[r, dx])
@@ -291,9 +306,7 @@
                 landed(ab.at[xs, r, cs], ac_recv.at[r, dx, dc])
         for p in range(pieces):
             cols = slice(p * nb, (p + 1) * nb)
-            gate = jnp.concatenate(
-                [mb[r + 1, b : b + 1, :] for b in range(p * nb // HD, (p + 1) * nb // HD)], axis=1
-            )
+            gate = gb[r + 1 : r + 2, cols]
             partial = 0.0
             for xs in range(G):
                 partial += jnp.dot(
@@ -324,6 +337,12 @@
                 def _():
                     up_out[r, p] = pb[r, p].astype(jnp.bfloat16)
                     up(r, p).start()
+
+    arrive(0)
+    for r in range(T - 1):
+        arrive(r + 1)
+        attend(r)
+        project(r)
 
     for r in reversed(range(2, T - 1)):
         for p in range(pieces):
@@ -365,20 +384,13 @@
 
     @pl.when(t == T - 1)
     def _():
-        copy = pltpu.make_async_copy(fresh_ref, out_ref, load_sem.at[2])
+        copy = pltpu.make_async_copy(fresh_ref, out_ref, load_sem.at[3])
         copy.start()
         copy.wait()
 
     for copy in meta_copies:
         copy.wait_send()
-    for dt, dx in others:
-        for kind in (1, 2):
-            outgoing(kind, dt, dx).wait_send()
-
-        @pl.when(t > 0)
-        def _():
-            outgoing(0, dt, dx).wait_send()
-
+    each_outgoing(lambda copy: copy.wait_send())
     for dc in range(1, C):
         for f in range(T):
             for xs in range(G):
@@ -414,17 +426,12 @@
         width = out_weight.shape[1]
         pieces = 2
         nb = width // pieces
-        gate = jnp.dot(
-            time_features(noise_steps), time_weight.astype(jnp.float32), precision=lax.Precision.HIGHEST
-        )
-        gate_rows = width // HD
-        meta_rows = -(-(gate_rows + T) // 8) * 8
-        mask_rows = jnp.broadcast_to(frame_mask[0].astype(jnp.float32)[:, None], (T, HD))
+        meta_rows = -(-(FREQ // HD + T) // 8) * 8
         meta = jnp.concatenate(
             [
-                gate.reshape(gate_rows, HD),
-                mask_rows,
-                jnp.zeros((meta_rows - gate_rows - T, HD), jnp.float32),
+                time_features(noise_steps).reshape(FREQ // HD, HD),
+                jnp.broadcast_to(frame_mask[0].astype(jnp.float32)[:, None], (T, HD)),
+                jnp.zeros((meta_rows - FREQ // HD - T, HD), jnp.float32),
             ],
             axis=0,
         )
@@ -435,7 +442,7 @@
         out = pl.pallas_call(
             functools.partial(fused_kernel, T, G, C, hp, pieces),
             out_shape=jax.ShapeDtypeStruct((tokens, width), bf16),
-            in_specs=[pl.BlockSpec(memory_space=pl.ANY)] * 7,
+            in_specs=[pl.BlockSpec(memory_space=pl.ANY)] * 8,
             out_specs=pl.BlockSpec(memory_space=pltpu.VMEM),
             scratch_shapes=[
                 pltpu.VMEM((T, G, tl, cw), bf16),
@@ -443,14 +450,17 @@
                 pltpu.VMEM((T, H, tl, cw), bf16),
                 pltpu.VMEM((G, T - 1, C, G * tl, cw), bf16),
                 pltpu.VMEM((T, meta_rows, HD), f32),
+                pltpu.VMEM((8, FREQ), f32),
+                pltpu.VMEM((8, width), f32),
                 pltpu.VMEM(out_weight.shape, bf16),
+                pltpu.VMEM(time_weight.shape, bf16),
                 pltpu.VMEM((tokens, width), bf16),
                 pltpu.VMEM(chunk, f32),
                 pltpu.VMEM(chunk, bf16),
                 pltpu.VMEM(chunk, bf16),
                 pltpu.VMEM(chunk, bf16),
                 pltpu.VMEM(chunk, bf16),
-                dma((3,)),
+                dma((4,)),
                 dma((T,)),
                 dma((T,)),
                 dma((3, T, G)),
@@ -469,7 +479,7 @@
             compiler_params=pltpu.CompilerParams(
                 collective_id=0, has_side_effects=True, vmem_limit_bytes=56 * 1024 * 1024
             ),
-        )(queries, keys, values, residual, fresh_frame, out_weight, meta)
+        )(queries, keys, values, residual, fresh_frame, out_weight, time_weight, meta)
         return out[None]
 
     return on_device_fused

time: 91.1 us -> 92.8 us (1.019)
  Pallas kernels: 84.7 us -> 88.4 us
  local copies, waits for them, and re-layouts: 3.45 us -> 2.12 us
    pallas_call x1, Pallas kernels: 84.7 us -> 88.4 us  [on_device_fused(): pl.pallas_call(functools.partial(fused_kernel, T, G, C, hp, pieces), out_...]
    unnamed x2 -> x1, local copies, waits for them, and re-layouts: 3.29 us -> 1.97 us
where the time goes in v2:
time: 92.8 us; the launch traced here: 92.6 us
  Pallas kernels  88.4 us (95%)
  local copies, waits for them, and re-layouts  2.12 us (2%)
  other arithmetic  1.38 us (1%)
    pallas_call x1, Pallas kernels, on_device_fused(): pl.pallas_call(functools.partial(fused_kernel, T, G, C, hp, pieces), out_...  88.4 us
    unnamed x1, local copies, waits for them, and re-layouts  1.97 us

profile of v2, /device:TPU:0, one launch (start us, length us, event | category | flops | bytes accessed | tf_op | source)
XLA Modules:
  0.0 92.6 jit_solution(2553956529811606744)
XLA Ops:
  0.7 0.7 convert_bitcast_fusion
  1.3 0.1 pad.1.clone
  1.4 0.1 pad.2.clone
  1.5 0.7 maximum_maximum_fusion.meta_ref
  2.2 88.4 %shard_map.91 = bf16[256,1280]{1,0:T(8,128)(2,1)} custom-call(bf16[1,64,3072]{2,1,0:T(8,128)(2,1)} %q_ref.1, bf16[1,64,3072]{2,1,0:T(8,128)(2,1)} %k_ref.1, bf16[1,64,3072]{2,1,0:T(8,128)(2,1)} %v_ref.1, bf16[1,256,1280]{2,1,0:T(8,128)(2,1)} %res_ref.1, bf16[256,1280]{1,0:T(8,128)(2,1)} %fresh_ref.1, bf16[768,1280]{1,0:T(8,128)(2,1)} %w_ref.1, ...), custom_call_target="tpu_custom_call" | custom-call | tf_op jit(solution)/shard_map/pallas_call | solution.py:442
  90.6 2.0 %copy.12 = bf16[1,256,1280]{2,1,0:T(8,128)(2,1)} copy(bf16[1,256,1280]{2,1,0:T(8,128)(2,1)} %bitcast.5) | data formatting | bytes 1310720
  (3 shorter events, 0.1 us)

commit v3 on v2

--- a/solution.py
+++ b/solution.py
@@ -294,12 +294,14 @@
             send_sem=up_send.at[r, p], recv_sem=up_recv.at[r, p], **to(t + 1, h),
         )
 
-    def project(r):
+    def hand_over(r):
         for dx in range(1, G):
             xs = lax.rem(x + G - dx, G)
             landed(ab.at[xs, r, c], ax_recv.at[r, dx])
             for dc in range(1, C):
                 aside(r, G - dx, dc).start()
+
+    def project(r):
         for dx in range(G):
             for dc in range(1, C):
                 xs, cs = lax.rem(x + dx, G), lax.rem(c + C - dc, C)
@@ -338,13 +340,7 @@
                     up_out[r, p] = pb[r, p].astype(jnp.bfloat16)
                     up(r, p).start()
 
-    arrive(0)
-    for r in range(T - 1):
-        arrive(r + 1)
-        attend(r)
-        project(r)
-
-    for r in reversed(range(2, T - 1)):
+    def relay_up(r):
         for p in range(pieces):
 
             @pl.when((t > 0) & (t < r))
@@ -353,7 +349,7 @@
                 up_out[r, p] = (pb[r, p] + up_in[r, p].astype(jnp.float32)).astype(jnp.bfloat16)
                 up(r, p).start()
 
-    for r in range(T - 2):
+    def relay_down(r):
         for p in range(pieces):
 
             @pl.when((t > r) & (t < T - 1))
@@ -363,6 +359,20 @@
                     jnp.bfloat16
                 )
                 down(r, p).start()
+
+    arrive(0)
+    for r in range(T - 1):
+        arrive(r + 1)
+        attend(r)
+        if r > 0:
+            hand_over(r - 1)
+            project(r - 1)
+    hand_over(T - 2)
+    project(T - 2)
+    for r in reversed(range(2, T - 1)):
+        relay_up(r)
+    for r in range(T - 2):
+        relay_down(r)
 
     for r in range(T - 1):
 
@@ -424,7 +434,7 @@
         tl = queries.shape[1]
         tokens = tl * H
         width = out_weight.shape[1]
-        pieces = 2
+        pieces = width // (2 * HD)
         nb = width // pieces
         meta_rows = -(-(FREQ // HD + T) // 8) * 8
         meta = jnp.concatenate(

time: 92.8 us -> 94 us (1.013)
  Pallas kernels: 88.4 us -> 89.6 us
    pallas_call x1, Pallas kernels: 88.4 us -> 89.6 us  [on_device_fused(): pl.pallas_call(functools.partial(fused_kernel, T, G, C, hp, pieces), out_...]
where the time goes in v3:
time: 94 us; the launch traced here: 93.8 us
  Pallas kernels  89.6 us (95%)
  local copies, waits for them, and re-layouts  2.12 us (2%)
  other arithmetic  1.38 us (1%)
    pallas_call x1, Pallas kernels, on_device_fused(): pl.pallas_call(functools.partial(fused_kernel, T, G, C, hp, pieces), out_...  89.6 us
    unnamed x1, local copies, waits for them, and re-layouts  1.97 us

profile of v3, /device:TPU:0, one launch (start us, length us, event | category | flops | bytes accessed | tf_op | source)
XLA Modules:
  0.0 93.8 jit_solution(7094906692241968924)
XLA Ops:
  0.7 0.7 convert_bitcast_fusion
  1.3 0.1 pad.1.clone
  1.4 0.1 pad.2.clone
  1.5 0.7 maximum_maximum_fusion.meta_ref
  2.2 89.6 %shard_map.91 = bf16[256,1280]{1,0:T(8,128)(2,1)} custom-call(bf16[1,64,3072]{2,1,0:T(8,128)(2,1)} %q_ref.1, bf16[1,64,3072]{2,1,0:T(8,128)(2,1)} %k_ref.1, bf16[1,64,3072]{2,1,0:T(8,128)(2,1)} %v_ref.1, bf16[1,256,1280]{2,1,0:T(8,128)(2,1)} %res_ref.1, bf16[256,1280]{1,0:T(8,128)(2,1)} %fresh_ref.1, bf16[768,1280]{1,0:T(8,128)(2,1)} %w_ref.1, ...), custom_call_target="tpu_custom_call" | custom-call | tf_op jit(solution)/shard_map/pallas_call | solution.py:452
  91.8 2.0 %copy.12 = bf16[1,256,1280]{2,1,0:T(8,128)(2,1)} copy(bf16[1,256,1280]{2,1,0:T(8,128)(2,1)} %bitcast.5) | data formatting | bytes 1310720
  (3 shorter events, 0.1 us)

commit v4 on v3

--- a/solution.py
+++ b/solution.py
@@ -100,12 +100,13 @@
 
 
 def fused_kernel(
-    T, G, C, hp, pieces,
+    T, G, C, hp, pieces, kept, groups,
     q_ref, k_ref, v_ref, res_ref, fresh_ref, w_ref, tw_ref, meta_ref,
     out_ref,
-    qb, kb, vb, ab, mb, fb, gb, wb, twb, rb, pb, down_out, down_in, up_out, up_in,
+    qb, kb, vb, ab, mb, fb, gb, wb, twb, rb, pb, down_out, down_in, up_out, up_in, ab3, w3,
     load_sem, meta_send, meta_recv, qkv_send, qkv_recv, pass_send, pass_recv,
     ax_send, ax_recv, ac_send, ac_recv, dn_send, dn_recv, up_send, up_recv,
+    w_send, w_recv, l_send, l_recv, lx_send, lx_recv, lc_send, lc_recv,
 ):
     t = lax.axis_index("tm")
     h = lax.axis_index("head")
@@ -122,6 +123,14 @@
     def to(tt, hh):
         return dict(device_id={"tm": tt, "head": hh}, device_id_type=pl.DeviceIdType.MESH)
 
+    group = lax.axis_index("groups")
+    share = w_ref.shape[0] // groups
+
+    def beside(dg):
+        return dict(
+            device_id={"groups": lax.rem(group + dg, groups)}, device_id_type=pl.DeviceIdType.MESH
+        )
+
     def landed(ref, sem):
         pltpu.make_async_copy(ref, ref, sem).wait()
 
@@ -142,7 +151,9 @@
         )
     for dc in range(1, C):
         pl.semaphore_signal(barrier, inc=1, **to(t, x * C + lax.rem(c + dc, C)))
-    pl.semaphore_wait(barrier, len(others) + C - 1)
+    for dg in range(1, groups):
+        pl.semaphore_signal(barrier, inc=1, **beside(dg))
+    pl.semaphore_wait(barrier, len(others) + C - 1 + groups - 1)
 
     own_meta = pltpu.make_async_copy(meta_ref, mb.at[t], meta_recv.at[t])
     own_meta.start()
@@ -165,11 +176,11 @@
         column = pl.multiple_of((tt * G + xx) * cw, HD)
         return sources[kind][0].at[0, :, pl.ds(column, cw)]
 
-    def outgoing(kind, tt, dx):
-        xx = lax.rem(x + dx, G)
+    def outgoing(kind, dt, dx):
+        tt, xx = lax.rem(t + dt, T), lax.rem(x + dx, G)
         return pltpu.make_async_remote_copy(
             src_ref=block(kind, tt, xx), dst_ref=slot(kind, t, x),
-            send_sem=qkv_send.at[kind, tt, dx], recv_sem=qkv_recv.at[kind, t, x],
+            send_sem=qkv_send.at[kind, dt, dx], recv_sem=qkv_recv.at[kind, t, x],
             **to(tt, xx * C + c),
         )
 
@@ -177,16 +188,31 @@
         return pltpu.make_async_copy(block(kind, t, x), slot(kind, t, x), qkv_recv.at[kind, t, x])
 
     def each_outgoing(act):
-        for tt in reversed(range(T)):
-            for dx in reversed(range(G)):
-                for kind in (1, 2, 0):
-                    wanted = t > 0 if kind == 0 else t >= 0
-                    if dx == 0:
-                        wanted = wanted & (t != tt)
-
-                    @pl.when(wanted)
-                    def _():
-                        act(outgoing(kind, tt, dx))
+        for dt, dx in others:
+            for kind in (1, 2):
+                act(outgoing(kind, dt, dx))
+
+            @pl.when(t > 0)
+            def _():
+                act(outgoing(0, dt, dx))
+
+    own_rows = pl.ds(group * share, share)
+
+    def lift_weight():
+        return pltpu.make_async_remote_copy(
+            src_ref=w_ref.at[own_rows, pl.ds(kept * nb, w3.shape[1])], dst_ref=w3.at[own_rows],
+            send_sem=w_send.at[0], recv_sem=w_recv.at[0], **to(t - 1, h),
+        )
+
+    def trade_weight(dg):
+        return pltpu.make_async_remote_copy(
+            src_ref=w3.at[own_rows], dst_ref=w3.at[own_rows],
+            send_sem=w_send.at[dg], recv_sem=w_recv.at[dg], **beside(dg),
+        )
+
+    @pl.when(t == T - 1)
+    def _():
+        lift_weight().start()
 
     each_outgoing(lambda copy: copy.start())
     for kind in (1, 2):
@@ -247,6 +273,58 @@
         )
 
     scale = 1.0 / math.sqrt(HD)
+
+    def lifted_up(r):
+        return pltpu.make_async_remote_copy(
+            src_ref=ab.at[x, r, c], dst_ref=ab3.at[x, r, c],
+            send_sem=l_send.at[r], recv_sem=l_recv.at[r], **to(t - 1, h),
+        )
+
+    def across3(r, dx):
+        xx = lax.rem(x + dx, G)
+        return pltpu.make_async_remote_copy(
+            src_ref=ab3.at[x, r, c], dst_ref=ab3.at[x, r, c],
+            send_sem=lx_send.at[r, dx], recv_sem=lx_recv.at[r, dx],
+            **to(t, xx * C + c),
+        )
+
+    def aside3(r, dx, dc):
+        xs = lax.rem(x + dx, G)
+        return pltpu.make_async_remote_copy(
+            src_ref=ab3.at[xs, r, c], dst_ref=ab3.at[xs, r, c],
+            send_sem=lc_send.at[r, dx, dc], recv_sem=lc_recv.at[r, dx, dc],
+            **to(t, x * C + lax.rem(c + dc, C)),
+        )
+
+    def spread3(r):
+        landed(ab3.at[x, r, c], l_recv.at[r])
+        for dx in range(1, G):
+            across3(r, dx).start()
+        for dc in range(1, C):
+            aside3(r, 0, dc).start()
+
+    def hand_over3(r):
+        for dx in range(1, G):
+            xs = lax.rem(x + G - dx, G)
+            landed(ab3.at[xs, r, c], lx_recv.at[r, dx])
+            for dc in range(1, C):
+                aside3(r, G - dx, dc).start()
+
+    def project3(r):
+        for dx in range(G):
+            for dc in range(1, C):
+                xs, cs = lax.rem(x + dx, G), lax.rem(c + C - dc, C)
+                landed(ab3.at[xs, r, cs], lc_recv.at[r, dx, dc])
+        for p in range(kept, pieces):
+            cols = slice((p - kept) * nb, (p - kept + 1) * nb)
+            partial = 0.0
+            for xs in range(G):
+                partial += jnp.dot(
+                    ab3[xs, r].reshape(tokens, cw),
+                    w3[xs * cw : (xs + 1) * cw, cols],
+                    preferred_element_type=jnp.float32,
+                )
+            pb[r, p] += partial * gb[r + 1 : r + 2, p * nb : (p + 1) * nb]
 
     def attend(r):
         f = r + 1
@@ -277,6 +355,12 @@
                 lifted.astype(jnp.bfloat16), value, preferred_element_type=jnp.float32
             )
             ab[x, r, c, :, cols] = (mixed / total).astype(jnp.bfloat16)
+        if r < T - 2:
+
+            @pl.when(t == T - 1)
+            def _():
+                lifted_up(r).start()
+
         for dx in range(1, G):
             across(r, dx).start()
         for dc in range(1, C):
@@ -328,10 +412,12 @@
                             jnp.float32
                         )
 
-            @pl.when(t == T - 1)
-            def _():
-                down_out[r, p] = pb[r, p].astype(jnp.bfloat16)
-                down(r, p).start()
+            if r == T - 2 or p < kept:
+
+                @pl.when(t == T - 1)
+                def _():
+                    down_out[r, p] = pb[r, p].astype(jnp.bfloat16)
+                    down(r, p).start()
 
             if r > 0:
 
@@ -352,7 +438,14 @@
     def relay_down(r):
         for p in range(pieces):
 
-            @pl.when((t > r) & (t < T - 1))
+            if p >= kept:
+
+                @pl.when(t == T - 2)
+                def _():
+                    down_out[r, p] = pb[r, p].astype(jnp.bfloat16)
+                    down(r, p).start()
+
+            @pl.when((t > r) & (t < (T - 2 if p >= kept else T - 1)))
             def _():
                 landed(down_in.at[r, p], dn_recv.at[r, p])
                 down_out[r, p] = (pb[r, p] + down_in[r, p].astype(jnp.float32)).astype(
@@ -364,11 +457,35 @@
     for r in range(T - 1):
         arrive(r + 1)
         attend(r)
+        if r == 0:
+
+            @pl.when(t == T - 2)
+            def _():
+                landed(w3.at[own_rows], w_recv.at[0])
+                for dg in range(1, groups):
+                    trade_weight(dg).start()
+
         if r > 0:
             hand_over(r - 1)
             project(r - 1)
+    @pl.when(t == T - 2)
+    def _():
+        for r in range(T - 2):
+            spread3(r)
+
     hand_over(T - 2)
     project(T - 2)
+
+    @pl.when(t == T - 2)
+    def _():
+        for r in range(T - 2):
+            hand_over3(r)
+        for dg in range(1, groups):
+            theirs = pl.ds(lax.rem(group + groups - dg, groups) * share, share)
+            landed(w3.at[theirs], w_recv.at[dg])
+        for r in range(T - 2):
+            project3(r)
+
     for r in reversed(range(2, T - 1)):
         relay_up(r)
     for r in range(T - 2):
@@ -401,6 +518,24 @@
     for copy in meta_copies:
         copy.wait_send()
     each_outgoing(lambda copy: copy.wait_send())
+
+    @pl.when(t == T - 1)
+    def _():
+        lift_weight().wait_send()
+        for r in range(T - 2):
+            lifted_up(r).wait_send()
+
+    @pl.when(t == T - 2)
+    def _():
+        for dg in range(1, groups):
+            trade_weight(dg).wait_send()
+        for r in range(T - 2):
+            for dx in range(1, G):
+                across3(r, dx).wait_send()
+            for dx in range(G):
+                for dc in range(1, C):
+                    aside3(r, dx, dc).wait_send()
+
     for dc in range(1, C):
         for f in range(T):
             for xs in range(G):
@@ -414,7 +549,7 @@
                 aside(r, dx, dc).wait_send()
         for p in range(pieces):
 
-            @pl.when(t > r)
+            @pl.when((t > r) if r == T - 2 or p < kept else (t > r) & (t < T - 1))
             def _():
                 down(r, p).wait_send()
 
@@ -423,7 +558,7 @@
                 up(r, p).wait_send()
 
 
-def fused(T, H, heads):
+def fused(T, H, heads, groups):
     def on_device_fused(
         queries, keys, values, residual, fresh_frame, out_weight, time_weight, noise_steps, frame_mask
     ):
@@ -436,6 +571,7 @@
         width = out_weight.shape[1]
         pieces = width // (2 * HD)
         nb = width // pieces
+        kept = 2 * pieces // 5
         meta_rows = -(-(FREQ // HD + T) // 8) * 8
         meta = jnp.concatenate(
             [
@@ -450,7 +586,7 @@
         dma = pltpu.SemaphoreType.DMA
         chunk = (T - 1, pieces, tokens, nb)
         out = pl.pallas_call(
-            functools.partial(fused_kernel, T, G, C, hp, pieces),
+            functools.partial(fused_kernel, T, G, C, hp, pieces, kept, groups),
             out_shape=jax.ShapeDtypeStruct((tokens, width), bf16),
             in_specs=[pl.BlockSpec(memory_space=pl.ANY)] * 8,
             out_specs=pl.BlockSpec(memory_space=pltpu.VMEM),
@@ -470,6 +606,8 @@
                 pltpu.VMEM(chunk, bf16),
                 pltpu.VMEM(chunk, bf16),
                 pltpu.VMEM(chunk, bf16),
+                pltpu.VMEM((G, T - 1, C, G * tl, cw), bf16),
+                pltpu.VMEM((level_heads * HD, (pieces - kept) * nb), bf16),
                 dma((4,)),
                 dma((T,)),
                 dma((T,)),
@@ -485,6 +623,14 @@
                 dma((T - 1, pieces)),
                 dma((T - 1, pieces)),
                 dma((T - 1, pieces)),
+                dma((groups,)),
+                dma((groups,)),
+                dma((T - 1,)),
+                dma((T - 1,)),
+                dma((T - 1, G)),
+                dma((T - 1, G)),
+                dma((T - 1, G, C)),
+                dma((T - 1, G, C)),
             ],
             compiler_params=pltpu.CompilerParams(
                 collective_id=0, has_side_effects=True, vmem_limit_bytes=56 * 1024 * 1024
@@ -510,9 +656,9 @@
     def whole(*args):
         frames, spread = mesh.shape["tm"], mesh.shape["head"]
         heads = args[0].shape[2] // HD
-        fits = 1 < frames <= 4 and heads % frames == 0 and args[5].shape[1] % (spread * 2 * HD) == 0
+        fits = 2 < frames <= 4 and heads % frames == 0 and args[5].shape[1] % (spread * 2 * HD) == 0
         return jax.shard_map(
-            fused(frames, spread, heads) if fits else on_device,
+            fused(frames, spread, heads, mesh.shape["groups"]) if fits else on_device,
             mesh=mesh,
             in_specs=placed,
             out_specs=P(("groups", "tm"), None, "head"),

time: 94 us -> 88.7 us (0.944); the launches traced: 93.8 us -> 87.5 us
  Pallas kernels: 89.6 us -> 83.3 us
    pallas_call x1, Pallas kernels: 89.6 us -> 83.3 us  [on_device_fused(): pl.pallas_call(functools.partial(fused_kernel, T, G, C, hp, pieces, kept,...]
where the time goes in v4:
time: 88.7 us; the launch traced here: 87.5 us
  Pallas kernels  83.3 us (94%)
  local copies, waits for them, and re-layouts  2.12 us (2%)
  other arithmetic  1.38 us (2%)
    pallas_call x1, Pallas kernels, on_device_fused(): pl.pallas_call(functools.partial(fused_kernel, T, G, C, hp, pieces, kept,...  83.3 us
    unnamed x1, local copies, waits for them, and re-layouts  1.97 us

profile of v4, /device:TPU:0, one launch (start us, length us, event | category | flops | bytes accessed | tf_op | source)
XLA Modules:
  0.0 87.5 jit_solution(17641305687031508071)
XLA Ops:
  0.7 0.7 convert_bitcast_fusion
  1.3 0.1 pad.1.clone
  1.4 0.1 pad.2.clone
  1.5 0.7 maximum_maximum_fusion.meta_ref
  2.2 83.3 %shard_map.91 = bf16[256,1280]{1,0:T(8,128)(2,1)} custom-call(bf16[1,64,3072]{2,1,0:T(8,128)(2,1)} %q_ref.1, bf16[1,64,3072]{2,1,0:T(8,128)(2,1)} %k_ref.1, bf16[1,64,3072]{2,1,0:T(8,128)(2,1)} %v_ref.1, bf16[1,256,1280]{2,1,0:T(8,128)(2,1)} %res_ref.1, bf16[256,1280]{1,0:T(8,128)(2,1)} %fresh_ref.1, bf16[768,1280]{1,0:T(8,128)(2,1)} %w_ref.1, ...), custom_call_target="tpu_custom_call" | custom-call | tf_op jit(solution)/shard_map/pallas_call | solution.py:588
  85.6 2.0 %copy.12 = bf16[1,256,1280]{2,1,0:T(8,128)(2,1)} copy(bf16[1,256,1280]{2,1,0:T(8,128)(2,1)} %bitcast.5) | data formatting | bytes 1310720
  (3 shorter events, 0.1 us)

commit v5 on v4

--- a/solution.py
+++ b/solution.py
@@ -483,12 +483,18 @@
         for dg in range(1, groups):
             theirs = pl.ds(lax.rem(group + groups - dg, groups) * share, share)
             landed(w3.at[theirs], w_recv.at[dg])
-        for r in range(T - 2):
+        project3(0)
+
+    relay_down(0)
+
+    @pl.when(t == T - 2)
+    def _():
+        for r in range(1, T - 2):
             project3(r)
 
     for r in reversed(range(2, T - 1)):
         relay_up(r)
-    for r in range(T - 2):
+    for r in range(1, T - 2):
         relay_down(r)
 
     for r in range(T - 1):

time: 88.7 us -> 87.3 us (0.984)
  the two profiles are of different devices: /device:TPU:0 before, /device:TPU:16 now
where the time goes in v5:
time: 87.3 us; the launch traced here: 87.1 us
  Pallas kernels  82.9 us (95%)
  local copies, waits for them, and re-layouts  2.12 us (2%)
  other arithmetic  1.38 us (2%)
    pallas_call x1, Pallas kernels, on_device_fused(): pl.pallas_call(functools.partial(fused_kernel, T, G, C, hp, pieces, kept,...  82.9 us
    unnamed x1, local copies, waits for them, and re-layouts  1.97 us

profile of v5, /device:TPU:16, one launch (start us, length us, event | category | flops | bytes accessed | tf_op | source)
XLA Modules:
  0.0 87.1 jit_solution(14795520587952774983)
XLA Ops:
  0.7 0.7 convert_bitcast_fusion
  1.3 0.1 pad.1.clone
  1.4 0.1 pad.2.clone
  1.5 0.7 maximum_maximum_fusion.meta_ref
  2.2 82.9 %shard_map.91 = bf16[256,1280]{1,0:T(8,128)(2,1)} custom-call(bf16[1,64,3072]{2,1,0:T(8,128)(2,1)} %q_ref.1, bf16[1,64,3072]{2,1,0:T(8,128)(2,1)} %k_ref.1, bf16[1,64,3072]{2,1,0:T(8,128)(2,1)} %v_ref.1, bf16[1,256,1280]{2,1,0:T(8,128)(2,1)} %res_ref.1, bf16[256,1280]{1,0:T(8,128)(2,1)} %fresh_ref.1, bf16[768,1280]{1,0:T(8,128)(2,1)} %w_ref.1, ...), custom_call_target="tpu_custom_call" | custom-call | tf_op jit(solution)/shard_map/pallas_call | solution.py:594
  85.1 2.0 %copy.12 = bf16[1,256,1280]{2,1,0:T(8,128)(2,1)} copy(bf16[1,256,1280]{2,1,0:T(8,128)(2,1)} %bitcast.5) | data formatting | bytes 1310720
  (3 shorter events, 0.1 us)
